TPU v7x, 32 devices: a whole 2x2x4 slice. The times are simulated.
32 devices in a mesh: row: 4 (over x, core), col: 4 (over z), depth: 2 (over y).
Axes of the slice: x: 2, y: 2, z: 4, core: 2. Of those that a mesh axis runs over, the one named last changes fastest.
Arguments:
- candidates: bfloat16 [4096, 512], P('row', ('col', 'depth')), may hold values from -6 to 6
- references: bfloat16 [16384, 512], P(('col', 'depth'), 'row'), may hold values from -6 to 6
- rates: float32 [16384], P(('col', 'depth')), may hold values from 0.15 to 1.5
Outputs:
- kernel: float32 [4096, 16384], P('row', ('col', 'depth'))
All inputs are finite; a program needn't handle non-finite values.
Results may differ from a plain program's by a relative error of at most 0.0003.
Values may be sent and summed in bfloat16 or wider, within the bound.
No kernel may reach another device: no remote copies, remote signals or barrier semaphores. Data moves between devices by JAX's collectives and lax.ppermute only.
A program may use at most 64 MiB of HBM per device.

v0:
```python
import jax
import jax.numpy as jnp
from jax import lax
from jax.sharding import PartitionSpec as P


def per_device(candidates, references, rates):
    paired = lax.all_gather(candidates, "depth", axis=1, tiled=True)
    panel = lax.all_gather(paired, "col", axis=1, tiled=True)
    width = panel.shape[1]
    cand_sq = jnp.sum(jnp.square(panel.astype(jnp.float32)), axis=1)
    ref_whole = lax.all_gather(references, "row", axis=1, tiled=True)
    gram = lax.dot_general(
        panel, ref_whole, (((1,), (1,)), ((), ())), preferred_element_type=jnp.float32
    )
    ref_sq = jnp.sum(jnp.square(ref_whole.astype(jnp.float32)), axis=1)
    distance = cand_sq[:, None] + ref_sq[None, :] - 2.0 * gram
    return jnp.exp(-rates[None, :] * distance / width)


def solution(mesh):
    placed = (P("row", ("col", "depth")), P(("col", "depth"), "row"), P(("col", "depth")))
    return jax.shard_map(
        per_device,
        mesh=mesh,
        in_specs=placed,
        out_specs=P("row", ("col", "depth")),
        check_vma=False,
    )
```

profile of v0, /device:TPU:0, one launch (start us, length us, event | category | flops | bytes accessed | tf_op | source)
XLA Modules:
  0.0 86.2 jit_solution(17966104002795301806)
XLA Ops:
  6.5 0.0 all-gather.3.cloned.1.call-start
  6.5 9.0 %all_gather.9 = bf16[1024,128]{0,1:T(8,128)(2,1)} all-gather(bf16[1024,64]{0,1:T(8,128)(2,1)} %param.3), channel_id=1, replica_groups=mesh['row'=4,'col'=4,'depth'=2] {'depth'}, dimensions={1}, use_global_device_ids=true | all-gather | bytes 393216 | tf_op jit(solution)/shard_map/all_gather | solution.py:8
  15.5 0.0 all-gather.3.cloned.1.call-update
  15.5 0.0 all-gather.5.cloned.1.call-start
  15.6 0.7 all-gather.5.cloned.1.call-update
  16.3 0.7 neg.4
  17.0 26.9 %all-gather.3.cloned.1.call-done = bf16[1024,512]{0,1:T(8,128)(2,1)} async-done(((bf16[1024,128]{0,1:T(8,128)(2,1)}), bf16[1024,512]{0,1:T(8,128)(2,1)}) %all-gather.3.cloned.1.call-update) | async-done | bytes 1048592 | tf_op jit(solution)/shard_map/all_gather | solution.py:9
  43.9 1.5 %multiply_reduce_fusion.1 = f32[1024]{0:T(1024)S(1)} fusion(bf16[1024,512]{0,1:T(8,128)(2,1)} %all-gather.3.cloned.1.call-done), kind=kLoop, calls=%fused_computation.2 | loop fusion | flops 1571840 | bytes 1052672 | tf_op jit(solution)/shard_map/reduce_sum | solution.py:11
  45.4 22.4 %all-gather.5.cloned.1.call-done = bf16[2048,512]{1,0:T(8,128)(2,1)} async-done(((bf16[2048,128]{1,0:T(8,128)(2,1)}), bf16[2048,512]{1,0:T(8,128)(2,1)}) %all-gather.5.cloned.1.call-update) | async-done | bytes 2097168 | tf_op jit(solution)/shard_map/all_gather | solution.py:12
  67.8 2.1 %multiply_reduce_fusion = f32[2048]{0:T(1024)S(1)} fusion(bf16[2048,512]{1,0:T(8,128)(2,1)} %all-gather.5.cloned.1.call-done), kind=kLoop, calls=%fused_computation.1 | loop fusion | flops 3143680 | bytes 2105344 | tf_op jit(solution)/shard_map/reduce_sum | solution.py:16
  69.9 9.5 %multiply_exponential_fusion = f32[1024,2048]{1,0:T(8,128)} fusion(bf16[1024,512]{0,1:T(8,128)(2,1)} %all-gather.3.cloned.1.call-done, bf16[2048,512]{1,0:T(8,128)(2,1)} %all-gather.5.cloned.1.call-done, f32[2048]{0:T(1024)S(1)} %multiply_reduce_fusion, f32[1024]{0:T(1024)S(1)} %multiply_reduce_fusion.1, f32[2048]{0:T(1024)S(1)} %neg.4), kind=kOutput, calls=%fused_computation | convolution fusion | flops 2157969408 | bytes 11554816 | tf_op jit(solution)/shard_map/dot_general | solution.py:13
Async XLA Ops:
  6.5 37.4 %all-gather.3.cloned.1.call-start = ((), (), s32[]{:S(2)}) async-start(), calls=%async_computation | async-start | bytes 1310720 | tf_op jit(solution)/shard_map/all_gather | solution.py:9
  15.5 52.3 %all-gather.5.cloned.1.call-start = ((), (), s32[]{:S(2)}) async-start(), calls=%async_computation.1 | async-start | bytes 2621440 | tf_op jit(solution)/shard_map/all_gather | solution.py:12
Sparse Core Ops, SparseCore 0:
  15.7 28.2 all-gather.2
  45.5 22.3 all-gather.4
where the time goes:
time: 86.5 us; the launch traced here: 86.2 us
  waiting for transfers between devices  50.1 us (58%)
  between operations  13.4 us (15%)
  matrix products  9.5 us (11%)
  blocking collectives  8.97 us (10%)
  other arithmetic  4.24 us (5%)
    all_gather x1, waiting for transfers between devices, per_device(): panel = lax.all_gather(paired, 'col', axis=1, tiled=True)  26.9 us
    all_gather x1, waiting for transfers between devices, per_device(): ref_whole = lax.all_gather(references, 'row', axis=1, tiled=True)  22.4 us
    dot_general x1, matrix products, per_device(): lax.dot_general(panel, ref_whole, (((1,), (1,)), ((), ())), preferred_ele...  9.5 us
    all_gather x1, blocking collectives, per_device(): paired = lax.all_gather(candidates, 'depth', axis=1, tiled=True)  8.97 us
    reduce_sum x1, other arithmetic, per_device(): ref_sq = jnp.sum(jnp.square(ref_whole.astype(jnp.float32)), axis=1)  2.07 us
  transfers between devices with their start and end apart: 2, of which 2 were waited for; matrix products, arithmetic and copies ran while one was open for 3% of the time, Pallas kernels for 0%

commit v1 on v0

--- a/solution.py
+++ b/solution.py
@@ -4,9 +4,23 @@
 from jax.sharding import PartitionSpec as P
 
 
+def guide_tails_up(local):
+    buffers = [local]
+    parts_n = lax.psum(1, axis_name="col")
+    for k in range(parts_n - 1):
+        f_next = lax.ppermute(
+            buffers[-1], "col", [(no, (no + 1) % parts_n) for no in range(parts_n)]
+        )
+        buffers.append(f_next)
+    block_out = jnp.concatenate(buffers[::-1], axis=1)
+    big = lax.axis_index("col")
+    local_out = jnp.roll(block_out, (big + 1) * local.shape[1], axis=1)
+    return local_out
+
+
 def per_device(candidates, references, rates):
     paired = lax.all_gather(candidates, "depth", axis=1, tiled=True)
-    panel = lax.all_gather(paired, "col", axis=1, tiled=True)
+    panel = guide_tails_up(paired)
     width = panel.shape[1]
     cand_sq = jnp.sum(jnp.square(panel.astype(jnp.float32)), axis=1)
     ref_whole = lax.all_gather(references, "row", axis=1, tiled=True)

time: 86.5 us -> 56.7 us (0.66)
  waiting for transfers between devices: 50.1 us -> 24.1 us
  matrix products: 9.5 us -> 6.42 us
  starting transfers between devices: 0.04 us -> 1.76 us
  blocking collectives: 8.97 us -> 7.39 us
  other arithmetic: 4.24 us -> 3.17 us
    all_gather x1 -> x0, waiting for transfers between devices: 26.9 us -> none  [per_device(): panel = lax.all_gather(paired, 'col', axis=1, tiled=True)]
    ppermute x0 -> x3, waiting for transfers between devices: none -> 23.4 us  [guide_tails_up(): lax.ppermute(buffers[-1], 'col', [(no, (no + 1) % parts_n) for no in rang...]
    all_gather x1, waiting for transfers between devices: 22.4 us -> 0.01 us  [per_device(): ref_whole = lax.all_gather(references, 'row', axis=1, tiled=True)]
    dot_general x1, matrix products: 9.5 us -> 6.42 us  [per_device(): lax.dot_general(panel, ref_whole, (((1,), (1,)), ((), ())), preferred_ele...]
    ppermute x0 -> x3, starting transfers between devices: none -> 1.76 us  [guide_tails_up(): lax.ppermute(buffers[-1], 'col', [(no, (no + 1) % parts_n) for no in rang...]
    all_gather x1, blocking collectives: 8.97 us -> 7.39 us  [per_device(): paired = lax.all_gather(candidates, 'depth', axis=1, tiled=True)]
    reduce_sum x1, other arithmetic: 1.47 us -> 0.25 us  [per_device(): cand_sq = jnp.sum(jnp.square(panel.astype(jnp.float32)), axis=1)]
  transfers between devices with their start and end apart: 2 -> 4, of which waited for: 2 -> 3; matrix products, arithmetic and copies ran while one was open for 3% -> 2% of each run, Pallas kernels for 0% -> 0%
where the time goes in v1:
time: 56.7 us; the launch traced here: 56.5 us
  waiting for transfers between devices  24.1 us (43%)
  between operations  13.5 us (24%)
  blocking collectives  7.39 us (13%)
  matrix products  6.42 us (11%)
  other arithmetic  3.17 us (6%)
  starting transfers between devices  1.76 us (3%)
    ppermute x3, waiting for transfers between devices, guide_tails_up(): lax.ppermute(buffers[-1], 'col', [(no, (no + 1) % parts_n) for no in rang...  23.4 us
    all_gather x1, blocking collectives, per_device(): paired = lax.all_gather(candidates, 'depth', axis=1, tiled=True)  7.39 us
    dot_general x1, matrix products, per_device(): lax.dot_general(panel, ref_whole, (((1,), (1,)), ((), ())), preferred_ele...  6.42 us
    reduce_sum x1, other arithmetic, per_device(): ref_sq = jnp.sum(jnp.square(ref_whole.astype(jnp.float32)), axis=1)  2.22 us
    ppermute x3, starting transfers between devices, guide_tails_up(): lax.ppermute(buffers[-1], 'col', [(no, (no + 1) % parts_n) for no in rang...  1.76 us
  transfers between devices with their start and end apart: 4, of which 3 were waited for; matrix products, arithmetic and copies ran while one was open for 2% of the time, Pallas kernels for 0%

profile of v1, /device:TPU:0, one launch (start us, length us, event | category | flops | bytes accessed | tf_op | source)
XLA Modules:
  0.0 56.5 jit_solution(5615000896357319532)
XLA Ops:
  6.5 0.0 all-gather.2.cloned.1.call-start
  6.5 0.7 %all-gather.2.cloned.1.call-update = ((bf16[2048,128]{1,0:T(8,128)(2,1)}), bf16[2048,512]{1,0:T(8,128)(2,1)}) async-update(((), (), s32[]{:S(2)}) %all-gather.2.cloned.1.call-start, bf16[2048,128]{1,0:T(8,128)(2,1)} %param.4) | async-update | bytes 3145752
  7.3 7.4 %all_gather.6 = bf16[1024,128]{0,1:T(8,128)(2,1)S(1)} all-gather(bf16[1024,64]{0,1:T(8,128)(2,1)} %param.3), channel_id=1, replica_groups=mesh['row'=4,'col'=4,'depth'=2] {'depth'}, dimensions={1}, use_global_device_ids=true | all-gather | bytes 393216 | tf_op jit(solution)/shard_map/all_gather | solution.py:22
  14.6 1.8 %collective-permute-start = (bf16[1024,128]{0,1:T(8,128)(2,1)S(1)}, bf16[1024,128]{0,1:T(8,128)(2,1)S(1)}, u32[]{:S(2)}, u32[]{:S(2)}) collective-permute-start(bf16[1024,128]{0,1:T(8,128)(2,1)S(1)} %all_gather.6), channel_id=1, source_target_pairs={{0,2},{2,4},{4,6},{6,0},{1,3},{3,5},{5,7},{7,1},{8,10},{10,12},{12... | collective-permute-start | bytes 786440 | tf_op jit(solution)/shard_map/ppermute | solution.py:11
  16.4 7.5 %collective-permute-done = bf16[1024,128]{0,1:T(8,128)(2,1)S(1)} collective-permute-done((bf16[1024,128]{0,1:T(8,128)(2,1)S(1)}, bf16[1024,128]{0,1:T(8,128)(2,1)S(1)}, u32[]{:S(2)}, u32[]{:S(2)}) %collective-permute-start) | collective-permute-done | bytes 262176 | tf_op jit(solution)/shard_map/ppermute | solution.py:11
  23.9 0.0 collective-permute-start.1
  23.9 8.4 %collective-permute-done.1 = bf16[1024,128]{0,1:T(8,128)(2,1)S(1)} collective-permute-done((bf16[1024,128]{0,1:T(8,128)(2,1)S(1)}, bf16[1024,128]{0,1:T(8,128)(2,1)S(1)}, u32[]{:S(2)}, u32[]{:S(2)}) %collective-permute-start.1) | collective-permute-done | bytes 262176 | tf_op jit(solution)/shard_map/ppermute | solution.py:11
  32.3 0.0 collective-permute-start.2
  32.3 0.7 %neg.4 = f32[2048]{0:T(1024)S(1)} negate(f32[2048]{0:T(1024)} %param.5) | non-fusion elementwise | flops 2048 | bytes 16384 | tf_op jit(solution)/shard_map/neg | solution.py:32
  33.0 7.5 %collective-permute-done.2 = bf16[1024,128]{0,1:T(8,128)(2,1)S(1)} collective-permute-done((bf16[1024,128]{0,1:T(8,128)(2,1)S(1)}, bf16[1024,128]{0,1:T(8,128)(2,1)S(1)}, u32[]{:S(2)}, u32[]{:S(2)}) %collective-permute-start.2) | collective-permute-done | bytes 262176 | tf_op jit(solution)/shard_map/ppermute | solution.py:11
  40.7 0.3 multiply_reduce_fusion.1
  40.9 0.0 all-gather.2.cloned.1.call-done
  41.0 0.0 copy-start
  41.0 2.2 %multiply_reduce_fusion = f32[2048]{0:T(1024)S(1)} fusion(bf16[2048,512]{1,0:T(8,128)(2,1)} %all-gather.2.cloned.1.call-done), kind=kLoop, calls=%fused_computation.1 | loop fusion | flops 3143680 | bytes 2105344 | tf_op jit(solution)/shard_map/reduce_sum | solution.py:30
  43.2 0.0 copy-done
  43.2 6.4 %multiply_exponential_fusion = f32[1024,2048]{1,0:T(8,128)} fusion(bf16[2048,512]{1,0:T(8,128)(2,1)S(1)} %copy-done, f32[2048]{0:T(1024)S(1)} %multiply_reduce_fusion, f32[1024]{0:T(1024)S(1)} %multiply_reduce_fusion.1, f32[2048]{0:T(1024)S(1)} %neg.4, bf16[1024,1024]{0,1:T(8,128)(2,1)S(1)} %constant_dynamic-update-slice_fusion, s32[]{:T(128)S(6)} %select_n.14), kind=kOutput, calls=%fused_computation | convolution fusion | flops 2157969408 | bytes 11554820 | tf_op jit(solution)/shard_map/dot_general | solution.py:27
  (8 shorter events, 0.2 us)
Async XLA Ops:
  6.5 34.4 %all-gather.2.cloned.1.call-start = ((), (), s32[]{:S(2)}) async-start(), calls=%async_computation | async-start | bytes 2621440 | tf_op jit(solution)/shard_map/all_gather | solution.py:26
  14.6 9.3 %collective-permute-start = (bf16[1024,128]{0,1:T(8,128)(2,1)S(1)}, bf16[1024,128]{0,1:T(8,128)(2,1)S(1)}, u32[]{:S(2)}, u32[]{:S(2)}) collective-permute-start(bf16[1024,128]{0,1:T(8,128)(2,1)S(1)} %all_gather.6), channel_id=1, source_target_pairs={{0,2},{2,4},{4,6},{6,0},{1,3},{3,5},{5,7},{7,1},{8,10},{10,12},{12... | collective-permute-start | bytes 786440 | tf_op jit(solution)/shard_map/ppermute | solution.py:11
  23.9 8.4 %collective-permute-start.1 = (bf16[1024,128]{0,1:T(8,128)(2,1)S(1)}, bf16[1024,128]{0,1:T(8,128)(2,1)S(1)}, u32[]{:S(2)}, u32[]{:S(2)}) collective-permute-start(bf16[1024,128]{0,1:T(8,128)(2,1)S(1)} %collective-permute-done), channel_id=1, source_target_pairs={{0,2},{2,4},{4,6},{6,0},{1,3},{3,5},{5,7},{7,1},{8,10},{10,12},{12... | collective-permute-start | bytes 786440 | tf_op jit(solution)/shard_map/ppermute | solution.py:11
  32.3 8.2 %collective-permute-start.2 = (bf16[1024,128]{0,1:T(8,128)(2,1)S(1)}, bf16[1024,128]{0,1:T(8,128)(2,1)S(1)}, u32[]{:S(2)}, u32[]{:S(2)}) collective-permute-start(bf16[1024,128]{0,1:T(8,128)(2,1)S(1)} %collective-permute-done.1), channel_id=1, source_target_pairs={{0,2},{2,4},{4,6},{6,0},{1,3},{3,5},{5,7},{7,1},{8,10},{10,12},{12... | collective-permute-start | bytes 786440 | tf_op jit(solution)/shard_map/ppermute | solution.py:11
  41.0 2.2 %copy-start = (bf16[2048,512]{1,0:T(8,128)(2,1)S(1)}, bf16[2048,512]{1,0:T(8,128)(2,1)}, u32[]{:S(2)}) copy-start(bf16[2048,512]{1,0:T(8,128)(2,1)} %all-gather.2.cloned.1.call-done) | copy-start | bytes 6291460
Sparse Core Ops, SparseCore 0:
  8.9 25.5 all-gather.1
